TPU v7x, 32 devices: a whole 2x2x4 slice. The times are simulated.
32 devices in a mesh: net: 2 (over core), dp: 2 (over x), depth: 8 (over z, y).
Axes of the slice: x: 2, y: 2, z: 4, core: 2. Of those that a mesh axis runs over, the one named last changes fastest.
Arguments:
- features: bfloat16 [2, 2, 16, 64, 16, 128], P('net', 'dp', None, 'depth'), may hold values from -16 to 16
- labels: int32 [2, 64, 16, 128], P('dp', 'depth'), may hold values from 0 to 7
- masks: int32 [2, 2, 64, 16, 128], P('net', 'dp', 'depth'), may hold values 0 or 1
- conv_kernel: bfloat16 [2, 27, 16, 16], P('net'), may hold values from -0.3125 to 0.3125
- conv_bias: float32 [2, 16], P('net'), may hold values from -3 to 3
- head_weight: bfloat16 [2, 8, 16], P('net'), may hold values from -1.5 to 1.5
- head_bias: float32 [2, 8], P('net'), may hold values from -3 to 3
Outputs:
- grad_input: bfloat16 [2, 2, 16, 64, 16, 128], P('net', 'dp', None, 'depth')
- grad_kernel: float32 [2, 27, 16, 16], P('net')
- grad_bias: float32 [2, 16], P('net')
- grad_head: float32 [2, 8, 16], P('net')
- grad_head_bias: float32 [2, 8], P('net')
All inputs are finite; a program needn't handle non-finite values. No bound on the sum of `masks` on one device may be relied on, other than what follows from the above.
Results may differ from a plain program's by a relative error of at most 0.0063.
Values may be sent and summed in bfloat16 or wider, within the bound.
No kernel may reach another device: no remote copies, remote signals or barrier semaphores. Data moves between devices by JAX's collectives and lax.ppermute only.
A program may use at most 64 MiB of HBM per device.

v0:
```python
import jax
import jax.numpy as jnp
from jax import lax
from jax.sharding import PartitionSpec as P


def with_halo(x, sides, width):
    for axis, dim in sides:
        size, length = (lax.axis_size(axis), x.shape[dim])
        up = [(i, (i + 1) % size) for i in range(size - 1)]
        down = [(j, i) for i, j in up]
        last = lax.slice_in_dim(x, length - width, length, axis=dim)
        initial = lax.slice_in_dim(x, 0, width, axis=dim)
        before = lax.ppermute(last, axis, up)
        after = lax.ppermute(initial, axis, down)
        x = jnp.concatenate([before, x, after], axis=dim)
    return x


def swapped(value, axis, distance):
    mask = 2**distance
    pairs = [(source, source ^ mask) for source in range(lax.axis_size(axis))]
    return lax.ppermute(value, axis, pairs)


def pad_sides(field):
    return jnp.pad(field, ((0, 0), (0, 0), (1, 1), (1, 1)))


def correlate(padded, kernel, planes, height, breadth):
    summed = jnp.zeros((kernel.shape[1], planes, height, breadth), jnp.float32)
    for t in range(27):
        first, second, third = (t // 9, t // 3 % 3, t % 3)
        window = padded[
            :, first : first + planes, second : second + height, third : third + breadth
        ]
        summed = summed + jnp.einsum(
            "oc,cdhw->odhw", kernel[t], window, preferred_element_type=jnp.float32
        )
    return summed


def transpose_correlate(grad_padded, kernel, planes, height, breadth):
    summed = jnp.zeros((kernel.shape[2], planes, height, breadth), jnp.float32)
    for t in range(27):
        first, second, third = (2 - t // 9, 2 - t // 3 % 3, 2 - t % 3)
        window = grad_padded[
            :, first : first + planes, second : second + height, third : third + breadth
        ]
        summed = summed + jnp.einsum(
            "oc,odhw->cdhw", kernel[t], window, preferred_element_type=jnp.float32
        )
    return summed


def kernel_products(pre_half, padded, planes, height, breadth):
    pieces = []
    for t in range(27):
        first, second, third = (t // 9, t // 3 % 3, t % 3)
        window = padded[
            :, first : first + planes, second : second + height, third : third + breadth
        ]
        pieces.append(
            jnp.einsum("odhw,cdhw->oc", pre_half, window, preferred_element_type=jnp.float32)
        )
    return jnp.stack(pieces)


def forward_head(padded, kernel, bias_vec, head_mat, head_off, label_map, planes, height, breadth):
    preact = correlate(padded, kernel, planes, height, breadth) + bias_vec[:, None, None, None]
    hidden = jnp.maximum(preact, 0.0).astype(jnp.bfloat16)
    logits = (
        jnp.einsum("kc,cdhw->kdhw", head_mat, hidden, preferred_element_type=jnp.float32)
        + head_off[:, None, None, None]
    )
    log_total = jnp.log(jnp.sum(jnp.exp(logits), axis=0))
    classes = jnp.arange(logits.shape[0], dtype=jnp.int32)
    onehot = (label_map[None] == classes[:, None, None, None]).astype(jnp.float32)
    cross_ent = log_total - jnp.sum(onehot * logits, axis=0)
    soft_probs = jnp.exp(logits - log_total[None])
    return (preact, hidden, cross_ent, soft_probs, onehot)


def backward_head(peer_weight, soft_probs, onehot, preact, head_mat):
    logit_grad = peer_weight[None] * (soft_probs - onehot)
    logit_half = logit_grad.astype(jnp.bfloat16)
    hidden_grad = jnp.einsum(
        "kc,kdhw->cdhw", head_mat, logit_half, preferred_element_type=jnp.float32
    )
    pre_grad = jnp.where(preact > 0.0, hidden_grad, 0.0)
    return (logit_grad, logit_half, pre_grad)


def body(features, labels, masks, conv_kernel, conv_bias, head_weight, head_bias):
    field = features[0, 0]
    label_map = labels[0]
    selection = masks[0, 0]
    kernel = conv_kernel[0]
    bias_vec = conv_bias[0]
    head_mat = head_weight[0]
    head_off = head_bias[0]
    planes, height, breadth = (field.shape[1], field.shape[2], field.shape[3])
    padded = pad_sides(with_halo(field, (("depth", 1),), 1))
    preact, hidden, cross_ent, soft_probs, onehot = forward_head(
        padded, kernel, bias_vec, head_mat, head_off, label_map, planes, height, breadth
    )
    offered = selection.astype(jnp.float32) * jnp.exp(-cross_ent)
    peer_weight = swapped(offered, "net", 0)
    logit_grad, logit_half, pre_grad = backward_head(
        peer_weight, soft_probs, onehot, preact, head_mat
    )
    pre_half = pre_grad.astype(jnp.bfloat16)
    grad_padded = pad_sides(with_halo(pre_half, (("depth", 1),), 1))
    input_grad = transpose_correlate(grad_padded, kernel, planes, height, breadth).astype(
        jnp.bfloat16
    )
    kernel_grad = kernel_products(pre_half, padded, planes, height, breadth)
    bias_grad = jnp.sum(pre_grad, axis=(1, 2, 3))
    head_grad = jnp.einsum("kdhw,cdhw->kc", logit_half, hidden, preferred_element_type=jnp.float32)
    offset_grad = jnp.sum(logit_grad, axis=(1, 2, 3))
    kernel_grad, bias_grad, head_grad, offset_grad = lax.psum(
        (kernel_grad, bias_grad, head_grad, offset_grad), ("dp", "depth")
    )
    inverse_count = 1.0 / (lax.axis_size("dp") * lax.axis_size("depth") * planes * height * breadth)
    return (
        input_grad[None, None],
        (kernel_grad * inverse_count)[None],
        (bias_grad * inverse_count)[None],
        (head_grad * inverse_count)[None],
        (offset_grad * inverse_count)[None],
    )


def solution(mesh):
    in_specs = (
        P("net", "dp", None, "depth", None, None),
        P("dp", "depth", None, None),
        P("net", "dp", "depth", None, None),
        P("net", None, None, None),
        P("net", None),
        P("net", None, None),
        P("net", None),
    )
    out_specs = (
        P("net", "dp", None, "depth", None, None),
        P("net", None, None, None),
        P("net", None),
        P("net", None, None),
        P("net", None),
    )
    return jax.shard_map(body, mesh=mesh, in_specs=in_specs, out_specs=out_specs, check_vma=False)
```

profile of v0, /device:TPU:0, one launch (start us, length us, event | category | flops | bytes accessed | tf_op | source)
XLA Modules:
  0.0 147.9 jit_solution(3590571253808474643)
XLA Ops:
  0.7 1.4 copy.209
  2.1 0.7 fusion.270
  2.8 4.9 %collective-permute-start = (bf16[16,1,16,128]{3,0,2,1:T(8,128)(2,1)}, bf16[16,1,16,128]{3,0,2,1:T(8,128)(2,1)S(1)}, u32[]{:S(2)}, u32[]{:S(2)}) collective-permute-start(bf16[16,1,16,128]{3,0,2,1:T(8,128)(2,1)} %get-tuple-element.20), channel_id=1, source_target_pairs={{0,1},{1,2},{2,3},{3,4},{4,5},{5,6},{6,7},{8,9},{9,10},{10,11},{11... | collective-permute-start | bytes 196616 | tf_op jit(solution)/shard_map/ppermute | solution.py:14
  7.6 1.3 collective-permute-start.1
  8.9 0.4 fusion.271
  9.5 0.4 fusion.228
  9.9 0.9 fusion.272
  11.9 1.0 copy.185
  12.9 1.0 copy.184
  14.0 1.0 copy.182
  15.0 1.0 copy.181
  16.0 1.0 copy.180
  17.0 1.0 copy.183
  18.0 1.0 copy.179
  21.4 0.7 fusion.10
  29.7 0.8 fusion.61
  31.2 0.8 fusion.63
  32.0 0.5 select_reduce_fusion
  33.0 1.2 collective-permute-done.2
  34.2 0.5 fusion.268
  35.0 0.5 fusion.226
  35.5 0.4 fusion.92
  35.9 0.4 fusion.91
  37.0 0.4 fusion.88
  37.8 0.4 fusion.86
  38.2 0.4 fusion.85
  39.0 0.4 fusion.83
  39.4 0.4 fusion.82
  40.1 0.4 fusion.80
  40.6 0.4 fusion.79
  41.3 0.4 fusion.77
  41.7 0.4 fusion.76
  42.5 0.4 fusion.74
  42.9 0.4 fusion.73
  44.0 0.4 fusion.70
  44.8 0.4 fusion.68
  45.2 0.4 fusion.67
  46.2 80.8 %all-reduce.2 = (f32[27,16,16]{2,1,0:T(8,128)S(1)}, f32[16]{0:T(128)S(1)}, f32[8,16]{1,0:T(8,128)S(1)}, f32[8]{0:T(128)S(1)}) all-reduce(f32[27,16,16]{2,1,0:T(8,128)S(1)} %fusion.67, f32[16]{0:T(128)S(1)} %get-tuple-element.16, f32[8,16]{1,0:T(8,128)S(1)} %convolution_bitcast_fusion.51, ...), channel_id=1, replica_groups=mesh['net'=2,'dp'=2,'depth'=8] {'dp','depth'}, use_global_device_ids=true, to_apply=%region_2.3 | all-reduce | flops 7064 | bytes 56512 | tf_op jit(solution)/shard_map/psum | solution.py:121
  127.0 0.6 multiply_bitcast_fusion.1
  127.6 0.5 multiply_bitcast_fusion.2
  128.2 1.3 collective-permute-start.4
  129.4 4.8 %collective-permute-start.3 = (bf16[16,1,16,128]{3,0,2,1:T(8,128)(2,1)S(1)}, bf16[16,1,16,128]{3,0,2,1:T(8,128)(2,1)S(1)}, u32[]{:S(2)}, u32[]{:S(2)}) collective-permute-start(bf16[16,1,16,128]{3,0,2,1:T(8,128)(2,1)S(1)} %get-tuple-element.18), channel_id=1, source_target_pairs={{0,1},{1,2},{2,3},{3,4},{4,5},{5,6},{6,7},{8,9},{9,10},{10,11},{11... | collective-permute-start | bytes 196616 | tf_op jit(solution)/shard_map/ppermute | solution.py:14
  134.2 0.5 multiply_bitcast_fusion.3
  134.7 0.8 copy.68
  135.9 0.7 select_maximum_fusion
  145.0 0.8 fusion.59
  146.2 0.8 fusion.66
  147.0 0.9 copy.67
  (103 shorter events, 25.4 us)
Async XLA Ops:
  0.6 31.4 %copy-start = (bf16[1,8,16]{2,1,0:T(8,128)(2,1)S(1)}, bf16[1,8,16]{2,1,0:T(8,128)(2,1)}, u32[]{:S(2)}) copy-start(bf16[1,8,16]{2,1,0:T(8,128)(2,1)} %param.12) | copy-start | bytes 772
  0.6 8.3 %copy-start.1 = (bf16[1,27,16,16]{1,3,2,0:T(8,128)(2,1)S(1)}, bf16[1,27,16,16]{1,3,2,0:T(8,128)(2,1)}, u32[]{:S(2)}) copy-start(bf16[1,27,16,16]{1,3,2,0:T(8,128)(2,1)} %param.10) | copy-start | bytes 41476
  2.1 7.4 %copy-start.2 = (bf16[1,1,16,8,16,128]{5,4,3,2,1,0:T(8,128)(2,1)S(1)}, bf16[1,1,16,8,16,128]{5,4,3,2,1,0:T(8,128)(2,1)}, u32[]{:S(2)}) copy-start(bf16[1,1,16,8,16,128]{5,4,3,2,1,0:T(8,128)(2,1)} %param.7) | copy-start | bytes 1572868
  2.8 18.6 %collective-permute-start = (bf16[16,1,16,128]{3,0,2,1:T(8,128)(2,1)}, bf16[16,1,16,128]{3,0,2,1:T(8,128)(2,1)S(1)}, u32[]{:S(2)}, u32[]{:S(2)}) collective-permute-start(bf16[16,1,16,128]{3,0,2,1:T(8,128)(2,1)} %get-tuple-element.20), channel_id=1, source_target_pairs={{0,1},{1,2},{2,3},{3,4},{4,5},{5,6},{6,7},{8,9},{9,10},{10,11},{11... | collective-permute-start | bytes 196616 | tf_op jit(solution)/shard_map/ppermute | solution.py:14
  7.6 13.8 %collective-permute-start.1 = (bf16[16,1,16,128]{3,0,2,1:T(8,128)(2,1)}, bf16[16,1,16,128]{3,0,2,1:T(8,128)(2,1)S(1)}, u32[]{:S(2)}, u32[]{:S(2)}) collective-permute-start(bf16[16,1,16,128]{3,0,2,1:T(8,128)(2,1)} %get-tuple-element.21), channel_id=1, source_target_pairs={{1,0},{2,1},{3,2},{4,3},{5,4},{6,5},{7,6},{9,8},{10,9},{11,10},{12... | collective-permute-start | bytes 196616 | tf_op jit(solution)/shard_map/ppermute | solution.py:15
  30.5 0.7 copy-start.5
  31.2 0.9 copy-start.3
  31.2 0.9 copy-start.6
  32.0 0.8 copy-start.4
  32.9 1.3 collective-permute-start.2
  128.2 7.4 %collective-permute-start.4 = (bf16[16,1,16,128]{3,0,2,1:T(8,128)(2,1)S(1)}, bf16[16,1,16,128]{3,0,2,1:T(8,128)(2,1)S(1)}, u32[]{:S(2)}, u32[]{:S(2)}) collective-permute-start(bf16[16,1,16,128]{3,0,2,1:T(8,128)(2,1)S(1)} %get-tuple-element.19), channel_id=1, source_target_pairs={{1,0},{2,1},{3,2},{4,3},{5,4},{6,5},{7,6},{9,8},{10,9},{11,10},{12... | collective-permute-start | bytes 196616 | tf_op jit(solution)/shard_map/ppermute | solution.py:15
  129.4 6.4 %collective-permute-start.3 = (bf16[16,1,16,128]{3,0,2,1:T(8,128)(2,1)S(1)}, bf16[16,1,16,128]{3,0,2,1:T(8,128)(2,1)S(1)}, u32[]{:S(2)}, u32[]{:S(2)}) collective-permute-start(bf16[16,1,16,128]{3,0,2,1:T(8,128)(2,1)S(1)} %get-tuple-element.18), channel_id=1, source_target_pairs={{0,1},{1,2},{2,3},{3,4},{4,5},{5,6},{6,7},{8,9},{9,10},{10,11},{11... | collective-permute-start | bytes 196616 | tf_op jit(solution)/shard_map/ppermute | solution.py:14
where the time goes:
time: 149 us; the launch traced here: 148 us
  blocking collectives  80.8 us (54%)
  matrix products  32.3 us (22%)
  local copies, waits for them, and re-layouts  16.6 us (11%)
  starting transfers between devices  12.3 us (8%)
  other arithmetic  3.33 us (2%)
  waiting for transfers between devices  1.57 us (1%)
    psum x1, blocking collectives, body(): lax.psum((kernel_grad, bias_grad, head_grad, offset_grad), ('dp', 'depth'))  80.8 us
    unnamed x44, local copies, waits for them, and re-layouts  14.6 us
    dot_general x27, matrix products, transpose_correlate(): jnp.einsum('oc,odhw->cdhw', kernel[t], window, preferred_element_type=jnp...  10.8 us
    dot_general x27, matrix products, kernel_products(): jnp.einsum('odhw,cdhw->oc', pre_half, window, preferred_element_type=jnp....  10.4 us
    dot_general x27, matrix products, correlate(): jnp.einsum('oc,cdhw->odhw', kernel[t], window, preferred_element_type=jnp...  9.82 us
    ppermute x2, starting transfers between devices, with_halo(): before = lax.ppermute(last, axis, up)  9.63 us
  transfers between devices with their start and end apart: 5, of which 2 were waited for; matrix products, arithmetic and copies ran while one was open for 9% of the time, Pallas kernels for 0%

commit v1 on v0

--- a/solution.py
+++ b/solution.py
@@ -119,7 +119,7 @@
     head_grad = jnp.einsum("kdhw,cdhw->kc", logit_half, hidden, preferred_element_type=jnp.float32)
     offset_grad = jnp.sum(logit_grad, axis=(1, 2, 3))
     kernel_grad, bias_grad, head_grad, offset_grad = lax.psum(
-        (kernel_grad, bias_grad, head_grad, offset_grad), ("dp", "depth")
+        lax.psum((kernel_grad, bias_grad, head_grad, offset_grad), "depth"), "dp"
     )
     inverse_count = 1.0 / (lax.axis_size("dp") * lax.axis_size("depth") * planes * height * breadth)
     return (

time: 149 us -> 120 us (0.81)
  blocking collectives: 80.8 us -> 52 us
    psum x1 -> x2, blocking collectives: 80.8 us -> 52 us  [the longest x1 41.3 us: body(): lax.psum((kernel_grad, bias_grad, head_grad, offset_grad), 'depth')]
  transfers between devices with their start and end apart: 5 -> 5, of which waited for: 2 -> 2; matrix products, arithmetic and copies ran while one was open for 9% -> 12% of each run, Pallas kernels for 0% -> 0%
where the time goes in v1:
time: 120 us; the launch traced here: 119 us
  blocking collectives  52 us (43%)
  matrix products  32.2 us (27%)
  local copies, waits for them, and re-layouts  16.6 us (14%)
  starting transfers between devices  12.3 us (10%)
  other arithmetic  3.33 us (3%)
  waiting for transfers between devices  1.57 us (1%)
    psum x1, blocking collectives, body(): lax.psum((kernel_grad, bias_grad, head_grad, offset_grad), 'depth')  41.3 us
    unnamed x44, local copies, waits for them, and re-layouts  14.6 us
    dot_general x27, matrix products, transpose_correlate(): jnp.einsum('oc,odhw->cdhw', kernel[t], window, preferred_element_type=jnp...  10.8 us
    psum x1, blocking collectives, body(): lax.psum(lax.psum((kernel_grad, bias_grad, head_grad, offset_grad), 'dept...  10.7 us
    dot_general x27, matrix products, kernel_products(): jnp.einsum('odhw,cdhw->oc', pre_half, window, preferred_element_type=jnp....  10.4 us
    dot_general x27, matrix products, correlate(): jnp.einsum('oc,cdhw->odhw', kernel[t], window, preferred_element_type=jnp...  9.82 us
    ppermute x2, starting transfers between devices, with_halo(): before = lax.ppermute(last, axis, up)  9.63 us
    ppermute x2, starting transfers between devices, with_halo(): after = lax.ppermute(initial, axis, down)  2.57 us
  transfers between devices with their start and end apart: 5, of which 2 were waited for; matrix products, arithmetic and copies ran while one was open for 12% of the time, Pallas kernels for 0%

profile of v1, /device:TPU:0, one launch (start us, length us, event | category | flops | bytes accessed | tf_op | source)
XLA Modules:
  0.0 119.1 jit_solution(9514706902660120994)
XLA Ops:
  0.7 1.4 %copy.209 = bf16[1,1,16,8,16,128]{5,2,4,3,1,0:T(8,128)(2,1)S(1)} copy(bf16[1,1,16,8,16,128]{5,4,3,2,1,0:T(8,128)(2,1)} %param.7) | data formatting | bytes 1048576 | tf_op args[0]
  2.1 0.7 fusion.270
  2.8 4.9 %collective-permute-start = (bf16[16,1,16,128]{3,0,2,1:T(8,128)(2,1)}, bf16[16,1,16,128]{3,0,2,1:T(8,128)(2,1)S(1)}, u32[]{:S(2)}, u32[]{:S(2)}) collective-permute-start(bf16[16,1,16,128]{3,0,2,1:T(8,128)(2,1)} %get-tuple-element.24), channel_id=1, source_target_pairs={{0,1},{1,2},{2,3},{3,4},{4,5},{5,6},{6,7},{8,9},{9,10},{10,11},{11... | collective-permute-start | bytes 196616 | tf_op jit(solution)/shard_map/ppermute | solution.py:14
  7.6 1.3 %collective-permute-start.1 = (bf16[16,1,16,128]{3,0,2,1:T(8,128)(2,1)}, bf16[16,1,16,128]{3,0,2,1:T(8,128)(2,1)S(1)}, u32[]{:S(2)}, u32[]{:S(2)}) collective-permute-start(bf16[16,1,16,128]{3,0,2,1:T(8,128)(2,1)} %get-tuple-element.25), channel_id=1, source_target_pairs={{1,0},{2,1},{3,2},{4,3},{5,4},{6,5},{7,6},{9,8},{10,9},{11,10},{12... | collective-permute-start | bytes 196616 | tf_op jit(solution)/shard_map/ppermute | solution.py:15
  9.5 0.4 fusion.228
  9.9 0.9 fusion.272
  11.9 1.0 copy.185
  12.9 1.0 copy.184
  14.0 1.0 copy.182
  15.0 1.0 copy.181
  16.0 1.0 copy.180
  17.0 1.0 copy.183
  18.0 1.0 copy.179
  21.4 0.7 fusion.10
  29.7 0.8 fusion.61
  31.2 0.8 fusion.63
  32.1 0.5 select_reduce_fusion
  33.0 1.2 %collective-permute-done.2 = f32[8,16,128]{2,1,0:T(8,128)S(1)} collective-permute-done((f32[8,16,128]{2,1,0:T(8,128)S(1)}, f32[8,16,128]{2,1,0:T(8,128)S(1)}, u32[]{:S(2)}, u32[]{:S(2)}) %collective-permute-start.2) | collective-permute-done | bytes 65568 | tf_op jit(solution)/shard_map/ppermute | solution.py:23
  34.2 0.5 fusion.268
  35.0 0.5 fusion.226
  35.5 0.4 fusion.92
  35.9 0.4 fusion.91
  37.0 0.4 fusion.88
  37.8 0.4 fusion.86
  38.2 0.4 fusion.85
  39.0 0.4 fusion.83
  39.4 0.4 fusion.82
  40.1 0.4 fusion.80
  40.6 0.4 fusion.79
  41.3 0.4 fusion.77
  41.8 0.4 fusion.76
  42.5 0.4 fusion.74
  42.9 0.4 fusion.73
  44.0 0.4 fusion.70
  44.8 0.4 fusion.68
  45.2 0.4 fusion.67
  46.2 41.3 %all-reduce.2 = (f32[27,16,16]{2,1,0:T(8,128)S(1)}, f32[16]{0:T(128)S(1)}, f32[8,16]{1,0:T(8,128)S(1)}, f32[8]{0:T(128)S(1)}) all-reduce(f32[27,16,16]{2,1,0:T(8,128)S(1)} %fusion.67, f32[16]{0:T(128)S(1)} %get-tuple-element.20, f32[8,16]{1,0:T(8,128)S(1)} %convolution_bitcast_fusion.51, ...), channel_id=1, replica_groups=mesh['net'=2,'dp'=2,'depth'=8] {'depth'}, use_global_device_ids=true, to_apply=%region_2.3 | all-reduce | flops 7064 | bytes 56512 | tf_op jit(solution)/shard_map/psum | solution.py:122
  87.5 10.7 %all-reduce.3 = (f32[27,16,16]{2,1,0:T(8,128)S(1)}, f32[16]{0:T(128)S(1)}, f32[8,16]{1,0:T(8,128)S(1)}, f32[8]{0:T(128)S(1)}) all-reduce(f32[27,16,16]{2,1,0:T(8,128)S(1)} %get-tuple-element.12, f32[16]{0:T(128)S(1)} %get-tuple-element.13, f32[8,16]{1,0:T(8,128)S(1)} %get-tuple-element.14, ...), channel_id=1, replica_groups=mesh['net'=2,'dp'=2,'depth'=8] {'dp'}, use_global_device_ids=true, to_apply=%region_3.4 | all-reduce | flops 7064 | bytes 56512 | tf_op jit(solution)/shard_map/psum | solution.py:121
  98.2 0.6 multiply_bitcast_fusion.1
  98.8 0.5 multiply_bitcast_fusion.2
  99.3 1.3 %collective-permute-start.4 = (bf16[16,1,16,128]{3,0,2,1:T(8,128)(2,1)S(1)}, bf16[16,1,16,128]{3,0,2,1:T(8,128)(2,1)S(1)}, u32[]{:S(2)}, u32[]{:S(2)}) collective-permute-start(bf16[16,1,16,128]{3,0,2,1:T(8,128)(2,1)S(1)} %get-tuple-element.23), channel_id=1, source_target_pairs={{1,0},{2,1},{3,2},{4,3},{5,4},{6,5},{7,6},{9,8},{10,9},{11,10},{12... | collective-permute-start | bytes 196616 | tf_op jit(solution)/shard_map/ppermute | solution.py:15
  100.6 4.8 %collective-permute-start.3 = (bf16[16,1,16,128]{3,0,2,1:T(8,128)(2,1)S(1)}, bf16[16,1,16,128]{3,0,2,1:T(8,128)(2,1)S(1)}, u32[]{:S(2)}, u32[]{:S(2)}) collective-permute-start(bf16[16,1,16,128]{3,0,2,1:T(8,128)(2,1)S(1)} %get-tuple-element.22), channel_id=1, source_target_pairs={{0,1},{1,2},{2,3},{3,4},{4,5},{5,6},{6,7},{8,9},{9,10},{10,11},{11... | collective-permute-start | bytes 196616 | tf_op jit(solution)/shard_map/ppermute | solution.py:14
  105.4 0.5 multiply_bitcast_fusion.3
  105.9 0.8 copy.68
  107.1 0.7 select_maximum_fusion
  116.2 0.8 fusion.59
  117.3 0.8 fusion.66
  118.2 0.9 copy.67
  (104 shorter events, 25.8 us)
Async XLA Ops:
  0.6 31.4 %copy-start = (bf16[1,8,16]{2,1,0:T(8,128)(2,1)S(1)}, bf16[1,8,16]{2,1,0:T(8,128)(2,1)}, u32[]{:S(2)}) copy-start(bf16[1,8,16]{2,1,0:T(8,128)(2,1)} %param.12) | copy-start | bytes 772
  0.6 8.3 %copy-start.1 = (bf16[1,27,16,16]{1,3,2,0:T(8,128)(2,1)S(1)}, bf16[1,27,16,16]{1,3,2,0:T(8,128)(2,1)}, u32[]{:S(2)}) copy-start(bf16[1,27,16,16]{1,3,2,0:T(8,128)(2,1)} %param.10) | copy-start | bytes 41476
  2.1 7.4 %copy-start.2 = (bf16[1,1,16,8,16,128]{5,4,3,2,1,0:T(8,128)(2,1)S(1)}, bf16[1,1,16,8,16,128]{5,4,3,2,1,0:T(8,128)(2,1)}, u32[]{:S(2)}) copy-start(bf16[1,1,16,8,16,128]{5,4,3,2,1,0:T(8,128)(2,1)} %param.7) | copy-start | bytes 1572868
  2.8 18.7 %collective-permute-start = (bf16[16,1,16,128]{3,0,2,1:T(8,128)(2,1)}, bf16[16,1,16,128]{3,0,2,1:T(8,128)(2,1)S(1)}, u32[]{:S(2)}, u32[]{:S(2)}) collective-permute-start(bf16[16,1,16,128]{3,0,2,1:T(8,128)(2,1)} %get-tuple-element.24), channel_id=1, source_target_pairs={{0,1},{1,2},{2,3},{3,4},{4,5},{5,6},{6,7},{8,9},{9,10},{10,11},{11... | collective-permute-start | bytes 196616 | tf_op jit(solution)/shard_map/ppermute | solution.py:14
  7.6 13.8 %collective-permute-start.1 = (bf16[16,1,16,128]{3,0,2,1:T(8,128)(2,1)}, bf16[16,1,16,128]{3,0,2,1:T(8,128)(2,1)S(1)}, u32[]{:S(2)}, u32[]{:S(2)}) collective-permute-start(bf16[16,1,16,128]{3,0,2,1:T(8,128)(2,1)} %get-tuple-element.25), channel_id=1, source_target_pairs={{1,0},{2,1},{3,2},{4,3},{5,4},{6,5},{7,6},{9,8},{10,9},{11,10},{12... | collective-permute-start | bytes 196616 | tf_op jit(solution)/shard_map/ppermute | solution.py:15
  30.5 0.7 copy-start.5
  31.2 0.9 copy-start.3
  31.2 0.9 copy-start.6
  32.0 0.8 copy-start.4
  32.9 1.3 %collective-permute-start.2 = (f32[8,16,128]{2,1,0:T(8,128)S(1)}, f32[8,16,128]{2,1,0:T(8,128)S(1)}, u32[]{:S(2)}, u32[]{:S(2)}) collective-permute-start(f32[8,16,128]{2,1,0:T(8,128)S(1)} %get-tuple-element.26), channel_id=1, source_target_pairs={{0,16},{16,0},{1,17},{17,1},{2,18},{18,2},{3,19},{19,3},{4,20},{20... | collective-permute-start | bytes 196616 | tf_op jit(solution)/shard_map/ppermute | solution.py:23
  99.3 7.4 %collective-permute-start.4 = (bf16[16,1,16,128]{3,0,2,1:T(8,128)(2,1)S(1)}, bf16[16,1,16,128]{3,0,2,1:T(8,128)(2,1)S(1)}, u32[]{:S(2)}, u32[]{:S(2)}) collective-permute-start(bf16[16,1,16,128]{3,0,2,1:T(8,128)(2,1)S(1)} %get-tuple-element.23), channel_id=1, source_target_pairs={{1,0},{2,1},{3,2},{4,3},{5,4},{6,5},{7,6},{9,8},{10,9},{11,10},{12... | collective-permute-start | bytes 196616 | tf_op jit(solution)/shard_map/ppermute | solution.py:15
  100.6 6.4 %collective-permute-start.3 = (bf16[16,1,16,128]{3,0,2,1:T(8,128)(2,1)S(1)}, bf16[16,1,16,128]{3,0,2,1:T(8,128)(2,1)S(1)}, u32[]{:S(2)}, u32[]{:S(2)}) collective-permute-start(bf16[16,1,16,128]{3,0,2,1:T(8,128)(2,1)S(1)} %get-tuple-element.22), channel_id=1, source_target_pairs={{0,1},{1,2},{2,3},{3,4},{4,5},{5,6},{6,7},{8,9},{9,10},{10,11},{11... | collective-permute-start | bytes 196616 | tf_op jit(solution)/shard_map/ppermute | solution.py:14
